TPU v7x, 256 devices: a whole 4x4x8 slice. The times are simulated.
256 devices in a mesh: seq: 64 (over x, z, core), tp: 4 (over y).
Axes of the slice: x: 4, y: 4, z: 8, core: 2. Of those that a mesh axis runs over, the one named last changes fastest.
Arguments:
- hidden_in: bfloat16 [16384, 1536], P('seq', 'tp'), may hold values from -6 to 6
- w_in_gate: float32 [1536, 3072], P('seq', 'tp'), may hold values from -0.15625 to 0.15625
- w_in_value: float32 [1536, 3072], P('seq', 'tp'), may hold values from -0.15625 to 0.15625
- w_in_shared: float32 [1536, 256], P('seq'), may hold values from -0.15625 to 0.15625
- w_in_step: float32 [1536, 48], P('seq', 'tp'), may hold values from -0.15625 to 0.15625
- conv_value: float32 [4, 3072], P(None, 'tp'), may hold values from -3 to 3
- conv_shared: float32 [4, 256], replicated, may hold values from -3 to 3
- dt_bias: float32 [48], P('tp'), may hold values from -4 to -2
- a_log: float32 [48], P('tp'), may hold values from -8 to 0
- skip_gain: float32 [48], P('tp'), may hold values from 0.6 to 4.8
- norm_gain: float32 [3072], P('tp'), may hold values from 0.1 to 1.9
- w_out: float32 [3072, 1536], P('tp', 'seq'), may hold values from -0.109375 to 0.109375
- prompt_lengths: int32 [8], replicated, may hold values from 1 to 8192, 16384 in all
- row_blocks: int32 [64], replicated, may hold values from 0 to 63, each once
Outputs:
- mixed_out: bfloat16 [16384, 1536], P('seq', 'tp')
Inputs may be any that keep to these rules, and one draw needn't show every extreme that they name: `prompt_lengths`: 8 lengths that sum to 16384, the longest exactly 8192. `row_blocks`: a permutation of the row blocks.
All inputs are finite; a program needn't handle non-finite values.
Results may differ from a plain program's by a relative error of at most 0.02.
Values may be sent and summed in bfloat16 or wider, within the bound.
No kernel may reach another device: no remote copies, remote signals or barrier semaphores. Data moves between devices by JAX's collectives and lax.ppermute only.
A program may use at most 128 MiB of HBM per device.

v0:
```python
import jax
import jax.numpy as jnp
from jax import lax
from jax.sharding import PartitionSpec as P

EPSILON = 1e-05
HIGHEST_PREC = lax.Precision.HIGHEST


def passed_along(block, axis, distance):
    devices = range(lax.axis_size(axis))
    route = [(i - distance, i) for i in devices if i - distance in devices]
    return lax.ppermute(block, axis, route)


def prefix_2(x, axis, combine, identity):
    count, here = (lax.axis_size(axis), lax.axis_index(axis))
    everything = jax.tree.map(
        lambda part, kind: lax.all_gather(part.astype(kind), axis), x, (jnp.bfloat16, jnp.bfloat16)
    )
    start = jax.tree.map(
        lambda part, zero: jnp.broadcast_to(jnp.asarray(zero, part.dtype), part.shape), x, identity
    )

    def turn(k, before):
        reached = k < here
        new = combine(
            before, jax.tree.map(lambda part, own: part[k].astype(own.dtype), everything, x)
        )
        return jax.tree.map(lambda a, b: jnp.where(reached, a, b), new, before)

    return lax.fori_loop(0, count, turn, start)


def segment_of(positions, doc_ends):
    return jnp.sum((positions[:, None] >= doc_ends[None, :]).astype(jnp.int32), axis=1)


def span_parts(values, b_half, c_half, steps_dt, decay_rates, segments, prev_seg):
    length = values.shape[0]
    b_rows = b_half.astype(jnp.float32)
    cumulative = jnp.cumsum(-steps_dt * decay_rates[None, :], axis=0)
    places = jnp.arange(length)
    causal = (places[:, None] >= places[None, :]) & (segments[:, None] == segments[None, :])
    gaps_log = jnp.where(causal[:, :, None], cumulative[:, None, :] - cumulative[None, :, :], 0.0)
    decays_in = jnp.where(causal[:, :, None], jnp.exp(gaps_log), 0.0)
    scores = jnp.dot(c_half, b_half.T, preferred_element_type=jnp.float32)
    weights = scores[:, :, None] * decays_in * steps_dt[None, :, :]
    intra_part = jnp.einsum("ijh,jhp->ihp", weights, values, precision=HIGHEST_PREC)
    carry_in = jnp.where((segments == prev_seg)[:, None], jnp.exp(cumulative), 0.0)
    tail_weight = (
        jnp.where(
            (segments == segments[-1])[:, None], jnp.exp(cumulative[-1][None, :] - cumulative), 0.0
        )
        * steps_dt
    )
    fresh_state = jnp.einsum("jh,jhp,jn->hpn", tail_weight, values, b_rows, precision=HIGHEST_PREC)
    keep_factor = jnp.where(segments[-1] == prev_seg, jnp.exp(cumulative[-1]), 0.0)
    return (intra_part, carry_in, fresh_state, keep_factor)


def combine(earlier, later):
    return (earlier[0] * later[0], later[0][:, None, None] * earlier[1] + later[1])


def on_device(
    hidden_in,
    w_in_gate,
    w_in_value,
    w_in_shared,
    w_in_step,
    conv_value,
    conv_shared,
    dt_bias,
    a_log,
    skip_gain,
    norm_gain,
    w_out,
    prompt_lengths,
    row_blocks,
):
    seq_count = lax.axis_size("seq")
    tokens_here = hidden_in.shape[0]
    edge_count = conv_value.shape[0] - 1
    gathered = lax.all_gather(hidden_in, "tp", axis=1, tiled=True)
    row_count = gathered.shape[0]
    model_width = gathered.shape[1]
    permuted = jnp.take(
        gathered.reshape(row_count, seq_count, model_width // seq_count), row_blocks, axis=1
    ).reshape(row_count, model_width)
    stored = (
        w_in_gate.astype(jnp.bfloat16),
        w_in_value.astype(jnp.bfloat16),
        w_in_shared.astype(jnp.bfloat16),
        w_in_step.astype(jnp.bfloat16),
    )
    pieces = (
        lax.all_gather(stored[0], "seq", axis=0, tiled=True),
        lax.all_gather(stored[1], "seq", axis=0, tiled=True),
        lax.all_gather(stored[2], "seq", axis=0, tiled=True),
        lax.all_gather(stored[3], "seq", axis=0, tiled=True),
    )
    projected = tuple(
        (
            jnp.dot(permuted, weight_piece, preferred_element_type=jnp.float32)
            for weight_piece in pieces
        )
    )
    gate_all, value_all, shared_all, raw_all = [result.astype(jnp.bfloat16) for result in projected]
    mixed_in = jnp.concatenate([value_all, shared_all], axis=1)
    edge_mix = passed_along(mixed_in[tokens_here - edge_count :], "seq", 1)
    doc_ends = jnp.cumsum(prompt_lengths)
    first_pos = lax.axis_index("seq") * tokens_here
    positions = first_pos + jnp.arange(tokens_here, dtype=jnp.int32)
    edge_positions = first_pos - edge_count + jnp.arange(edge_count, dtype=jnp.int32)
    segments = segment_of(positions, doc_ends)
    ext_segments = jnp.concatenate([segment_of(edge_positions, doc_ends), segments])
    ext_rows = jnp.concatenate([edge_mix, mixed_in], axis=0)
    kernel = jnp.concatenate([conv_value, conv_shared], axis=1)
    conv_sum = jnp.zeros(mixed_in.shape, jnp.float32)
    for tap_index in range(edge_count + 1):
        same_doc = (ext_segments[tap_index : tap_index + tokens_here] == segments)[:, None]
        conv_sum = conv_sum + jnp.where(
            same_doc,
            kernel[tap_index][None, :]
            * ext_rows[tap_index : tap_index + tokens_here].astype(jnp.float32),
            0.0,
        )
    convolved = jax.nn.silu(conv_sum).astype(jnp.bfloat16)
    local_inner = conv_value.shape[1]
    local_heads = dt_bias.shape[0]
    head_dim = local_inner // local_heads
    state_size = conv_shared.shape[1] // 2
    values = (
        convolved[:, :local_inner].astype(jnp.float32).reshape(tokens_here, local_heads, head_dim)
    )
    b_half = convolved[:, local_inner : local_inner + state_size]
    c_half = convolved[:, local_inner + state_size :]
    c_rows = c_half.astype(jnp.float32)
    steps_dt = jax.nn.softplus(raw_all.astype(jnp.float32) + dt_bias[None, :])
    decay_rates = jnp.exp(a_log)
    prev_first = segment_of(jnp.reshape(first_pos - 1, (1,)), doc_ends)[0]
    device_keep = jnp.ones((local_heads,), jnp.float32)
    device_state = jnp.zeros((local_heads, head_dim, state_size), jnp.float32)
    parts = span_parts(values, b_half, c_half, steps_dt, decay_rates, segments, prev_first)
    device_keep = parts[3] * device_keep
    device_state = parts[3][:, None, None] * device_state + parts[2]
    identity = (jnp.ones_like(device_keep), jnp.zeros_like(device_state))
    prefix = prefix_2((device_keep, device_state), "seq", combine, identity)
    carried = prefix[1]
    intra_part, carry_in, fresh_state, keep_factor = parts
    inter_part = (
        jnp.einsum("in,hpn->ihp", c_rows, carried, precision=HIGHEST_PREC) * carry_in[:, :, None]
    )
    outputs = intra_part + inter_part
    mixed_heads = outputs + skip_gain[None, :, None] * values
    gated = mixed_heads.reshape(tokens_here, local_inner) * jax.nn.silu(
        gate_all.astype(jnp.float32)
    )
    squares = jnp.sum(gated * gated, axis=1)
    square_total = lax.psum(squares, "tp")
    mean_square = square_total / (local_inner * lax.axis_size("tp"))
    normed = (gated * lax.rsqrt(mean_square + EPSILON)[:, None] * norm_gain[None, :]).astype(
        jnp.bfloat16
    )
    out_weight = w_out.astype(jnp.bfloat16)
    partial_terms = jnp.dot(
        normed,
        lax.all_gather(out_weight, "seq", axis=1, tiled=True),
        preferred_element_type=jnp.float32,
    )
    return lax.psum_scatter(
        partial_terms.astype(jnp.bfloat16), "tp", scatter_dimension=1, tiled=True
    )


def solution(mesh):
    return jax.shard_map(
        on_device,
        mesh=mesh,
        in_specs=(
            P("seq", "tp"),
            P("seq", "tp"),
            P("seq", "tp"),
            P("seq", None),
            P("seq", "tp"),
            P(None, "tp"),
            P(),
            P("tp"),
            P("tp"),
            P("tp"),
            P("tp"),
            P("tp", "seq"),
            P(),
            P(),
        ),
        out_specs=P("seq", "tp"),
        check_vma=False,
    )
```

profile of v0, /device:TPU:2, one launch (start us, length us, event | category | flops | bytes accessed | tf_op | source)
XLA Modules:
  0.0 420.0 jit_solution(3729731392679539498)
XLA Ops:
  6.5 1.5 convert_element_type.112
  9.6 1.1 copy.39
  13.0 46.7 %all-gather.1 = bf16[64,24,12]{1,2,0:T(8,128)(2,1)S(1)} all-gather(bf16[1,24,12]{1,2,0:T(8,128)(2,1)S(1)} %convert_bitcast_fusion), channel_id=1, replica_groups=mesh['seq'=64,'tp'=4] {'seq'}, dimensions={0}, use_global_device_ids=true | all-gather | bytes 37440 | tf_op jit(solution)/shard_map/all_gather | solution.py:101
  61.4 14.2 %all_gather.28 = bf16[256,1536]{0,1:T(8,128)(2,1)S(1)} all-gather(bf16[256,384]{0,1:T(8,128)(2,1)S(1)} %copy.39), channel_id=1, replica_groups=mesh['seq'=64,'tp'=4] {'tp'}, dimensions={1}, use_global_device_ids=true | all-gather | bytes 983040 | tf_op jit(solution)/shard_map/all_gather | solution.py:85
  80.0 48.3 %all_gather.30 = bf16[1536,256]{1,0:T(8,128)(2,1)S(1)} all-gather(bf16[24,256]{1,0:T(8,128)(2,1)S(1)} %convert_element_type.114), channel_id=1, replica_groups=mesh['seq'=64,'tp'=4] {'seq'}, dimensions={0}, use_global_device_ids=true | all-gather | bytes 798720 | tf_op jit(solution)/shard_map/all_gather | solution.py:100
  128.3 1.3 broadcast_compare_fusion
  130.1 2.5 convolution_convert_fusion.2
  132.6 2.3 collective-permute-start
  134.9 4.8 %collective-permute-done = bf16[3,1024]{1,0:T(4,128)(2,1)S(1)} collective-permute-done((bf16[3,1024]{1,0:T(4,128)(2,1)S(1)}, bf16[3,1024]{1,0:T(4,128)(2,1)S(1)}, u32[]{:S(2)}, u32[]{:S(2)}) %collective-permute-start) | collective-permute-done | bytes 6176 | tf_op jit(solution)/shard_map/ppermute | solution.py:13
  140.9 1.2 fusion.20
  143.9 38.1 %all-gather.2 = bf16[64,1,12]{2,1,0:T(2,128)(2,1)S(1)} all-gather(bf16[1,1,12]{2,1,0:T(2,128)(2,1)S(1)} %bitcast.96), channel_id=1, replica_groups=mesh['seq'=64,'tp'=4] {'seq'}, dimensions={0}, use_global_device_ids=true | all-gather | bytes 1560 | tf_op jit(solution)/shard_map/all_gather | solution.py:19
  182.2 3.6 fusion.14
  185.8 43.4 %all-gather.14.cloned.1.call-done = bf16[768,64,128]{2,1,0:T(8,128)(2,1)} async-done(((bf16[12,64,128]{2,1,0:T(8,128)(2,1)}), bf16[768,64,128]{2,1,0:T(8,128)(2,1)}) %all-gather.14.cloned.1.call-update) | async-done | bytes 12582928 | tf_op jit(solution)/shard_map/all_gather | solution.py:19
  229.1 70.1 %while.14 = (s32[]{:T(128)}, f32[12,64,128]{2,1,0:T(8,128)S(1)}, s32[]{:T(128)}, bf16[64,12]{1,0:T(8,128)(2,1)S(1)}, bf16[64,12,64,128]{3,2,1,0:T(8,128)(2,1)}, /*index=5*/s32[]{:T(128)}, s32[]{:T(128)}) while((s32[]{:T(128)}, f32[12,64,128]{2,1,0:T(8,128)S(1)}, s32[]{:T(128)}, bf16[64,12]{1,0:T(8,128)(2,1)S(1)}, ...), condition=%wide.region_7.8_spmd.clone, body=%wide.region_6.7_spmd.clone.sunk | while | flops 491536 | bytes 983265 | solution.py:32
  229.2 1.1 fusion.58
  230.2 1.1 fusion.58
  231.3 1.1 fusion.58
  233.5 1.1 fusion.58
  234.6 1.1 fusion.58
  235.7 1.1 fusion.58
  236.8 1.1 fusion.58
  237.9 1.1 fusion.58
  239.0 1.1 fusion.58
  240.1 1.1 fusion.58
  241.2 1.1 fusion.58
  242.3 1.1 fusion.58
  244.5 1.1 fusion.58
  245.6 1.1 fusion.58
  246.7 1.1 fusion.58
  247.7 1.1 fusion.58
  248.8 1.1 fusion.58
  249.9 1.1 fusion.58
  251.0 1.1 fusion.58
  252.1 1.1 fusion.58
  253.2 1.1 fusion.58
  254.3 1.1 fusion.58
  255.4 1.1 fusion.58
  256.5 1.1 fusion.58
  257.6 1.1 fusion.58
  258.7 1.1 fusion.58
  259.8 1.1 fusion.58
  260.9 1.1 fusion.58
  262.0 1.1 fusion.58
  263.1 1.1 fusion.58
  264.2 1.1 fusion.58
  265.3 1.1 fusion.58
  266.3 1.1 fusion.58
  267.4 1.1 fusion.58
  268.5 1.1 fusion.58
  278.4 1.1 fusion.58
  283.9 1.1 fusion.58
  287.2 1.1 fusion.58
  294.9 1.1 fusion.58
  296.0 1.1 fusion.58
  298.2 1.1 fusion.58
  299.3 1.6 fusion.18
  301.2 5.5 %all-gather.10.cloned.1.call-done = bf16[1536,768]{1,0:T(8,128)(2,1)} async-done(((bf16[24,768]{1,0:T(8,128)(2,1)}), bf16[1536,768]{1,0:T(8,128)(2,1)}) %all-gather.10.cloned.1.call-update) | async-done | bytes 2359312 | tf_op jit(solution)/shard_map/all_gather | solution.py:98
  306.7 2.7 multiply_reduce_fusion
  309.4 10.5 %psum.7 = f32[256]{0:T(256)S(1)} all-reduce(f32[256]{0:T(256)S(1)} %get-tuple-element.160), channel_id=1, replica_groups=mesh['seq'=64,'tp'=4] {'tp'}, use_global_device_ids=true, to_apply=%region_9.10 | all-reduce | flops 256 | bytes 2048 | tf_op jit(solution)/shard_map/psum | solution.py:161
  319.8 64.6 %all-gather.12.cloned.1.call-done = bf16[768,1536]{0,1:T(8,128)(2,1)} async-done(((bf16[768,24]{0,1:T(8,128)(2,1)}), bf16[768,1536]{0,1:T(8,128)(2,1)}) %all-gather.12.cloned.1.call-update) | async-done | bytes 2359312 | tf_op jit(solution)/shard_map/all_gather | solution.py:169
  384.4 2.5 convolution_convert_fusion
  386.9 1.2 copy.50
  388.1 23.7 %reduce-scatter.4.cloned.1.call-done = bf16[384,256]{1,0:T(8,128)(2,1)} async-done(((bf16[1536,256]{1,0:T(8,128)(2,1)}), bf16[384,256]{1,0:T(8,128)(2,1)}) %reduce-scatter.4.cloned.1.call-update) | async-done | bytes 196624
  411.8 1.7 copy.51
  (164 shorter events, 37.4 us)
Async XLA Ops:
  6.5 123.6 %all-gather.8.cloned.1.call-start = ((), (), s32[]{:S(2)}) async-start(), calls=%async_computation.1 | async-start | bytes 2396160 | tf_op jit(solution)/shard_map/all_gather | solution.py:99
  8.1 221.1 %all-gather.14.cloned.1.call-start = ((), (), s32[]{:S(2)}) async-start(), calls=%async_computation.4 | async-start | bytes 12779520 | tf_op jit(solution)/shard_map/all_gather | solution.py:19
  75.6 0.9 copy-start.5
  76.2 3.6 copy-start.2
  76.2 3.6 copy-start.4
  132.6 7.1 %collective-permute-start = (bf16[3,1024]{1,0:T(4,128)(2,1)S(1)}, bf16[3,1024]{1,0:T(4,128)(2,1)S(1)}, u32[]{:S(2)}, u32[]{:S(2)}) collective-permute-start(bf16[3,1024]{1,0:T(4,128)(2,1)S(1)} %fusion.40), channel_id=1, source_target_pairs={{0,4},{4,8},{8,12},{12,16},{16,20},{20,24},{24,28},{28,32},{32,36}... | collective-permute-start | bytes 18440 | tf_op jit(solution)/shard_map/ppermute | solution.py:13
  139.9 2.3 copy-start
  139.9 3.1 copy-start.1
  142.2 164.5 %all-gather.10.cloned.1.call-start = ((), (), s32[]{:S(2)}) async-start(), calls=%async_computation.2 | async-start | bytes 2396160 | tf_op jit(solution)/shard_map/all_gather | solution.py:98
  142.9 241.5 %all-gather.12.cloned.1.call-start = ((), (), s32[]{:S(2)}) async-start(), calls=%async_computation.3 | async-start | bytes 2396160 | tf_op jit(solution)/shard_map/all_gather | solution.py:169
  143.6 268.2 %reduce-scatter.4.cloned.1.call-start = ((), (), s32[]{:S(2)}) async-start(), calls=%async_computation.5 | async-start | bytes 983040
  229.1 70.1 %copy-start.6 = (f32[12]{0:T(128)S(1)}, f32[12]{0:T(128)}, u32[]{:S(2)}) copy-start(f32[12]{0:T(128)} %param.25) | copy-start | bytes 148
  301.2 83.2 %copy-start.3 = (f32[768]{0:T(1024)S(1)}, f32[768]{0:T(1024)}, u32[]{:S(2)}) copy-start(f32[768]{0:T(1024)} %param.26) | copy-start | bytes 9220
Sparse Core Ops, SparseCore 0:
  10.1 79.4 all-gather.7
  142.3 86.8 all-gather.13
  231.8 74.7 all-gather.9
  309.2 75.1 all-gather.11
  388.2 23.5 reduce-scatter.3
where the time goes:
time: 422 us; the launch traced here: 420 us
  blocking collectives  158 us (37%)
  waiting for transfers between devices  142 us (34%)
  other arithmetic  79 us (19%)
  matrix products  14.9 us (4%)
  between operations  14.6 us (3%)
  local copies, waits for them, and re-layouts  7.21 us (2%)
    select_n x64, other arithmetic, turn(): return jax.tree.map(lambda a, b: jnp.where(reached, a, b), new, before)  67.4 us
    all_gather x1, waiting for transfers between devices, on_device(): lax.all_gather(out_weight, 'seq', axis=1, tiled=True)  64.6 us
    all_gather x1, blocking collectives, on_device(): lax.all_gather(stored[2], 'seq', axis=0, tiled=True)  48.3 us
    all_gather x1, blocking collectives, on_device(): lax.all_gather(stored[3], 'seq', axis=0, tiled=True)  46.7 us
    all_gather x1, waiting for transfers between devices, prefix_2(): lax.all_gather(part.astype(kind), axis)  43.4 us
    all_gather x1, blocking collectives, prefix_2(): lax.all_gather(part.astype(kind), axis)  38.1 us
    unnamed x6, waiting for transfers between devices  23.8 us
    all_gather x1, blocking collectives, on_device(): gathered = lax.all_gather(hidden_in, 'tp', axis=1, tiled=True)  14.2 us
  transfers between devices with their start and end apart: 6, of which 5 were waited for; matrix products, arithmetic and copies ran while one was open for 21% of the time, Pallas kernels for 0%

commit v1 on v0

--- a/solution.py
+++ b/solution.py
@@ -158,7 +158,8 @@
         gate_all.astype(jnp.float32)
     )
     squares = jnp.sum(gated * gated, axis=1)
-    square_total = lax.psum(squares, "tp")
+    shards = lax.all_gather(squares, "tp", axis=0, tiled=False)
+    square_total = shards.sum(axis=0)
     mean_square = square_total / (local_inner * lax.axis_size("tp"))
     normed = (gated * lax.rsqrt(mean_square + EPSILON)[:, None] * norm_gain[None, :]).astype(
         jnp.bfloat16

time: 422 us -> 422 us (level)
    psum x1 -> x0, blocking collectives: 10.5 us -> none  [on_device(): square_total = lax.psum(squares, 'tp')]
    all_gather x0 -> x1, blocking collectives: none -> 9.71 us  [on_device(): shards = lax.all_gather(squares, 'tp', axis=0, tiled=False)]
where the time goes in v1:
time: 422 us; the launch traced here: 420 us
  blocking collectives  157 us (37%)
  waiting for transfers between devices  143 us (34%)
  other arithmetic  79 us (19%)
  matrix products  14.9 us (4%)
  between operations  14.6 us (3%)
  local copies, waits for them, and re-layouts  7.21 us (2%)
    select_n x64, other arithmetic, turn(): return jax.tree.map(lambda a, b: jnp.where(reached, a, b), new, before)  67.4 us
    all_gather x1, waiting for transfers between devices, on_device(): lax.all_gather(out_weight, 'seq', axis=1, tiled=True)  65.3 us
    all_gather x1, blocking collectives, on_device(): lax.all_gather(stored[2], 'seq', axis=0, tiled=True)  48.3 us
    all_gather x1, blocking collectives, on_device(): lax.all_gather(stored[3], 'seq', axis=0, tiled=True)  46.7 us
    all_gather x1, waiting for transfers between devices, prefix_2(): lax.all_gather(part.astype(kind), axis)  43.4 us
    all_gather x1, blocking collectives, prefix_2(): lax.all_gather(part.astype(kind), axis)  38.1 us
    unnamed x6, waiting for transfers between devices  23.8 us
    all_gather x1, blocking collectives, on_device(): gathered = lax.all_gather(hidden_in, 'tp', axis=1, tiled=True)  14.2 us
  transfers between devices with their start and end apart: 6, of which 5 were waited for; matrix products, arithmetic and copies ran while one was open for 21% of the time, Pallas kernels for 0%

profile of v1, /device:TPU:2, one launch (start us, length us, event | category | flops | bytes accessed | tf_op | source)
XLA Modules:
  0.0 420.0 jit_solution(11364080849285243726)
XLA Ops:
  6.5 1.5 convert_element_type.112
  9.6 1.1 copy.39
  13.0 46.7 %all-gather.2 = bf16[64,24,12]{1,2,0:T(8,128)(2,1)S(1)} all-gather(bf16[1,24,12]{1,2,0:T(8,128)(2,1)S(1)} %convert_bitcast_fusion), channel_id=1, replica_groups=mesh['seq'=64,'tp'=4] {'seq'}, dimensions={0}, use_global_device_ids=true | all-gather | bytes 37440 | tf_op jit(solution)/shard_map/all_gather | solution.py:101
  61.4 14.2 %all_gather.34 = bf16[256,1536]{0,1:T(8,128)(2,1)S(1)} all-gather(bf16[256,384]{0,1:T(8,128)(2,1)S(1)} %copy.39), channel_id=1, replica_groups=mesh['seq'=64,'tp'=4] {'tp'}, dimensions={1}, use_global_device_ids=true | all-gather | bytes 983040 | tf_op jit(solution)/shard_map/all_gather | solution.py:85
  80.0 48.3 %all_gather.36 = bf16[1536,256]{1,0:T(8,128)(2,1)S(1)} all-gather(bf16[24,256]{1,0:T(8,128)(2,1)S(1)} %convert_element_type.114), channel_id=1, replica_groups=mesh['seq'=64,'tp'=4] {'seq'}, dimensions={0}, use_global_device_ids=true | all-gather | bytes 798720 | tf_op jit(solution)/shard_map/all_gather | solution.py:100
  128.3 1.3 broadcast_compare_fusion
  130.1 2.5 convolution_convert_fusion.2
  132.6 2.3 collective-permute-start
  134.9 4.8 %collective-permute-done = bf16[3,1024]{1,0:T(4,128)(2,1)S(1)} collective-permute-done((bf16[3,1024]{1,0:T(4,128)(2,1)S(1)}, bf16[3,1024]{1,0:T(4,128)(2,1)S(1)}, u32[]{:S(2)}, u32[]{:S(2)}) %collective-permute-start) | collective-permute-done | bytes 6176 | tf_op jit(solution)/shard_map/ppermute | solution.py:13
  140.9 1.2 fusion.20
  143.9 38.1 %all-gather.3 = bf16[64,1,12]{2,1,0:T(2,128)(2,1)S(1)} all-gather(bf16[1,1,12]{2,1,0:T(2,128)(2,1)S(1)} %bitcast.97), channel_id=1, replica_groups=mesh['seq'=64,'tp'=4] {'seq'}, dimensions={0}, use_global_device_ids=true | all-gather | bytes 1560 | tf_op jit(solution)/shard_map/all_gather | solution.py:19
  182.2 3.6 fusion.14
  185.8 43.4 %all-gather.16.cloned.1.call-done = bf16[768,64,128]{2,1,0:T(8,128)(2,1)} async-done(((bf16[12,64,128]{2,1,0:T(8,128)(2,1)}), bf16[768,64,128]{2,1,0:T(8,128)(2,1)}) %all-gather.16.cloned.1.call-update) | async-done | bytes 12582928 | tf_op jit(solution)/shard_map/all_gather | solution.py:19
  229.1 70.1 %while.14 = (s32[]{:T(128)}, f32[12,64,128]{2,1,0:T(8,128)S(1)}, s32[]{:T(128)}, bf16[64,12]{1,0:T(8,128)(2,1)S(1)}, bf16[64,12,64,128]{3,2,1,0:T(8,128)(2,1)}, /*index=5*/s32[]{:T(128)}, s32[]{:T(128)}) while((s32[]{:T(128)}, f32[12,64,128]{2,1,0:T(8,128)S(1)}, s32[]{:T(128)}, bf16[64,12]{1,0:T(8,128)(2,1)S(1)}, ...), condition=%wide.region_7.8_spmd.clone, body=%wide.region_6.7_spmd.clone.sunk | while | flops 491536 | bytes 983265 | solution.py:32
  229.2 1.1 fusion.58
  230.2 1.1 fusion.58
  231.3 1.1 fusion.58
  233.5 1.1 fusion.58
  234.6 1.1 fusion.58
  235.7 1.1 fusion.58
  236.8 1.1 fusion.58
  237.9 1.1 fusion.58
  239.0 1.1 fusion.58
  240.1 1.1 fusion.58
  241.2 1.1 fusion.58
  242.3 1.1 fusion.58
  244.5 1.1 fusion.58
  245.6 1.1 fusion.58
  246.7 1.1 fusion.58
  247.7 1.1 fusion.58
  248.8 1.1 fusion.58
  249.9 1.1 fusion.58
  251.0 1.1 fusion.58
  252.1 1.1 fusion.58
  253.2 1.1 fusion.58
  254.3 1.1 fusion.58
  255.4 1.1 fusion.58
  256.5 1.1 fusion.58
  257.6 1.1 fusion.58
  258.7 1.1 fusion.58
  259.8 1.1 fusion.58
  260.9 1.1 fusion.58
  262.0 1.1 fusion.58
  263.1 1.1 fusion.58
  264.2 1.1 fusion.58
  265.3 1.1 fusion.58
  266.3 1.1 fusion.58
  267.4 1.1 fusion.58
  268.5 1.1 fusion.58
  278.4 1.1 fusion.58
  283.9 1.1 fusion.58
  287.2 1.1 fusion.58
  294.9 1.1 fusion.58
  296.0 1.1 fusion.58
  298.2 1.1 fusion.58
  299.3 1.6 fusion.18
  301.2 5.5 %all-gather.12.cloned.1.call-done = bf16[1536,768]{1,0:T(8,128)(2,1)} async-done(((bf16[24,768]{1,0:T(8,128)(2,1)}), bf16[1536,768]{1,0:T(8,128)(2,1)}) %all-gather.12.cloned.1.call-update) | async-done | bytes 2359312 | tf_op jit(solution)/shard_map/all_gather | solution.py:98
  306.7 2.7 multiply_reduce_fusion
  309.4 9.7 %all-gather.4 = f32[4,1,256]{2,1,0:T(1,128)S(1)} all-gather(f32[1,1,256]{2,1,0:T(1,128)S(1)} %bitcast.98), channel_id=3, replica_groups=mesh['seq'=64,'tp'=4] {'tp'}, dimensions={0}, use_global_device_ids=true | all-gather | bytes 5120 | tf_op jit(solution)/shard_map/all_gather | solution.py:161
  319.1 65.3 %all-gather.14.cloned.1.call-done = bf16[768,1536]{0,1:T(8,128)(2,1)} async-done(((bf16[768,24]{0,1:T(8,128)(2,1)}), bf16[768,1536]{0,1:T(8,128)(2,1)}) %all-gather.14.cloned.1.call-update) | async-done | bytes 2359312 | tf_op jit(solution)/shard_map/all_gather | solution.py:170
  384.4 2.5 convolution_convert_fusion
  386.9 1.2 copy.50
  388.1 23.7 %reduce-scatter.4.cloned.1.call-done = bf16[384,256]{1,0:T(8,128)(2,1)} async-done(((bf16[1536,256]{1,0:T(8,128)(2,1)}), bf16[384,256]{1,0:T(8,128)(2,1)}) %reduce-scatter.4.cloned.1.call-update) | async-done | bytes 196624
  411.8 1.7 copy.51
  (165 shorter events, 37.4 us)
Async XLA Ops:
  6.5 123.6 %all-gather.10.cloned.1.call-start = ((), (), s32[]{:S(2)}) async-start(), calls=%async_computation.1 | async-start | bytes 2396160 | tf_op jit(solution)/shard_map/all_gather | solution.py:99
  8.1 221.1 %all-gather.16.cloned.1.call-start = ((), (), s32[]{:S(2)}) async-start(), calls=%async_computation.4 | async-start | bytes 12779520 | tf_op jit(solution)/shard_map/all_gather | solution.py:19
  75.6 0.9 copy-start.5
  76.2 3.6 copy-start.2
  76.2 3.6 copy-start.4
  132.6 7.1 %collective-permute-start = (bf16[3,1024]{1,0:T(4,128)(2,1)S(1)}, bf16[3,1024]{1,0:T(4,128)(2,1)S(1)}, u32[]{:S(2)}, u32[]{:S(2)}) collective-permute-start(bf16[3,1024]{1,0:T(4,128)(2,1)S(1)} %fusion.40), channel_id=1, source_target_pairs={{0,4},{4,8},{8,12},{12,16},{16,20},{20,24},{24,28},{28,32},{32,36}... | collective-permute-start | bytes 18440 | tf_op jit(solution)/shard_map/ppermute | solution.py:13
  139.9 2.3 copy-start
  139.9 3.1 copy-start.1
  142.2 164.5 %all-gather.12.cloned.1.call-start = ((), (), s32[]{:S(2)}) async-start(), calls=%async_computation.2 | async-start | bytes 2396160 | tf_op jit(solution)/shard_map/all_gather | solution.py:98
  142.9 241.5 %all-gather.14.cloned.1.call-start = ((), (), s32[]{:S(2)}) async-start(), calls=%async_computation.3 | async-start | bytes 2396160 | tf_op jit(solution)/shard_map/all_gather | solution.py:170
  143.6 268.2 %reduce-scatter.4.cloned.1.call-start = ((), (), s32[]{:S(2)}) async-start(), calls=%async_computation.5 | async-start | bytes 983040
  229.1 70.1 %copy-start.6 = (f32[12]{0:T(128)S(1)}, f32[12]{0:T(128)}, u32[]{:S(2)}) copy-start(f32[12]{0:T(128)} %param.25) | copy-start | bytes 148
  301.2 83.2 %copy-start.3 = (f32[768]{0:T(1024)S(1)}, f32[768]{0:T(1024)}, u32[]{:S(2)}) copy-start(f32[768]{0:T(1024)} %param.26) | copy-start | bytes 9220
Sparse Core Ops, SparseCore 0:
  10.1 79.4 all-gather.9
  142.3 86.8 all-gather.15
  231.8 74.7 all-gather.11
  309.2 75.1 all-gather.13
  388.2 23.5 reduce-scatter.3
